TPU v7x, 32 devices: a whole 2x2x4 slice. The times are simulated.
32 devices in a mesh: vol: 8 (over z, x), nar: 4 (over y, core).
Axes of the slice: x: 2, y: 2, z: 4, core: 2. Of those that a mesh axis runs over, the one named last changes fastest.
Arguments:
- series: bfloat16 [2048, 2048], P(('vol', 'nar')), may hold values from -6 to 6
- send_rows: int32 [8, 4, 16], P('vol', 'nar'), may hold values from -1 to 63, as said below
- bin_counts: int32 [4], replicated, may hold values from 1 to 128, 256 in all
- observer_cells: int32 [2, 512], replicated, may hold values from 0 to 127
Outputs:
- spectra_out: float32 [4, 128, 2, 512], P('nar', 'vol')
Inputs may be any that keep to these rules, and one draw needn't show every extreme that they name: `send_rows`: entry (u, n, k) names the row of device (u, n)'s 64 rows of series for slot k mod 2 bound for the patch owner at vol index k // 2 and nar index n, or is -1 for an empty slot; one device never names a row twice. Nar index m owns bin_counts[m] bins in order, from the sum of the counts before m on; some owner holds exactly 128 bins. `observer_cells`: row 0 holds polar indices, row 1 azimuthal indices.
All inputs are finite; a program needn't handle non-finite values.
Results may differ from a plain program's by a relative error of at most 0.0043.
Values may be sent and summed in bfloat16 or wider, within the bound.
No kernel may reach another device: no remote copies, remote signals or barrier semaphores. Data moves between devices by JAX's collectives and lax.ppermute only.
A program may use at most 64 MiB of HBM per device.

v0:
```python
import math
import jax
import jax.numpy as jnp
from jax import lax
from jax.sharding import PartitionSpec as P

NF = 256
NQ = 4
WAVE_STEP = 0.05


def dft_table(bin_ids, keep_bin, time_len):
    time_steps = jnp.arange(time_len, dtype=jnp.int32)
    frequency = bin_ids + 1
    phase_turns = time_steps[:, None] * frequency[None, :] % time_len
    angle_grid = phase_turns.astype(jnp.float32) * (2.0 * math.pi / time_len)
    dft_grid = jnp.stack([jnp.cos(angle_grid), -jnp.sin(angle_grid)], axis=-1)
    dft_grid = jnp.where(keep_bin[None, :, None], dft_grid, jnp.float32(0.0))
    return dft_grid.reshape(time_len, 2 * bin_ids.shape[0]).astype(jnp.bfloat16)


def positions(point_list):
    beside_all = (point_list * 1597 % 8191).astype(jnp.float32) * (2.0 * math.pi / 8191.0)
    jitter = (point_list * 613 % 127).astype(jnp.float32) * (0.37 / 127.0)
    axial = (point_list // 128).astype(jnp.float32) * 0.5 + jitter
    return (20.0 * jnp.cos(beside_all), 20.0 * jnp.sin(beside_all), axial)


def directions(obs_cells):
    polar_angle = (obs_cells[0].astype(jnp.float32) + 0.5) * (math.pi / 128.0)
    azimuth = obs_cells[1].astype(jnp.float32) * (2.0 * math.pi / 128.0)
    return (
        jnp.sin(polar_angle) * jnp.cos(azimuth),
        jnp.sin(polar_angle) * jnp.sin(azimuth),
        jnp.cos(polar_angle),
    )


def project(facing, place_xyz):
    dotted = facing[0][:, None] * place_xyz[0][None, :] + facing[1][:, None] * place_xyz[1][None, :]
    return dotted + facing[2][:, None] * place_xyz[2][None, :]


def kernels(bin_ids, dotted):
    wavenumber = (bin_ids.astype(jnp.float32) + 1.0) * WAVE_STEP
    phase_grid = wavenumber[:, None, None] * dotted[None]
    return jnp.concatenate([jnp.cos(phase_grid), jnp.sin(phase_grid)], axis=1).astype(jnp.bfloat16)


def combine(products, bin_ids, facing, norm_scale):
    observers = facing[0].shape[0]
    bin_total = bin_ids.shape[0]
    cos_part = products[:, :observers].reshape(bin_total, observers, NQ, 2)
    sine_part = products[:, observers:].reshape(bin_total, observers, NQ, 2)
    real_part = cos_part[..., 0] + sine_part[..., 1]
    imag_part = cos_part[..., 1] - sine_part[..., 0]
    weights = jnp.stack([jnp.ones_like(facing[0]), facing[0], facing[1], facing[2]], axis=-1)
    real_sum = jnp.sum(real_part * weights[None], axis=-1)
    imag_sum = jnp.sum(imag_part * weights[None], axis=-1)
    amplitude = (bin_ids.astype(jnp.float32) + 1.0) * (norm_scale / NF)
    return jnp.stack([-amplitude[:, None] * imag_sum, amplitude[:, None] * real_sum], axis=1)


def apply_green(bin_ids, spec_block, dotted, facing, norm_scale):
    green_grid = kernels(bin_ids, dotted)
    products = jnp.einsum(
        "bxp,bcp->bxc", green_grid, spec_block, preferred_element_type=jnp.float32
    )
    return combine(products, bin_ids, facing, norm_scale)


def per_device(series, send_rows, bin_counts, observer_cells):
    vol_count = lax.axis_size("vol")
    nar_count = lax.axis_size("nar")
    vol_index = lax.axis_index("vol")
    nar_index = lax.axis_index("nar")
    bin_cap = vol_count * max(1, 2 * NF // (nar_count * vol_count))
    time_len = series.shape[1] // NQ
    slot_total = send_rows.shape[2]
    slot_width = slot_total // vol_count
    listing = send_rows.reshape(-1)
    picked = jnp.take(series, jnp.maximum(listing, 0), axis=0)
    packed = jnp.where((listing >= 0)[:, None], picked, jnp.zeros((), series.dtype))
    arrived = lax.all_to_all(packed, "vol", split_axis=0, concat_axis=0, tiled=True)
    starts = jnp.cumsum(bin_counts) - bin_counts
    own_start = starts[nar_index]
    own_count = bin_counts[nar_index]
    dft_scale = 1.0 / math.sqrt(time_len)
    within = jnp.arange(bin_cap, dtype=jnp.int32)
    own_table = dft_table(own_start + within, within < own_count, time_len)
    row_piece = lax.all_gather(arrived, "nar", axis=0, tiled=True)
    rows_here = row_piece.shape[0]
    spectral = jnp.dot(
        row_piece.reshape(rows_here * NQ, time_len), own_table, preferred_element_type=jnp.float32
    )
    spectral = (spectral * dft_scale).astype(jnp.bfloat16).reshape(rows_here, NQ, bin_cap, 2)
    spectra = spectral.transpose(2, 1, 3, 0).reshape(bin_cap, 2 * NQ, rows_here)
    local_points = nar_count * slot_total

    def point_ids(vol_owner, flat_index):
        nar_source = flat_index // slot_total
        remain = flat_index % slot_total
        vol_source = remain // slot_width
        within_slot = remain % slot_width
        return (
            (vol_source * nar_count + nar_source) * vol_count + vol_owner
        ) * slot_width + within_slot

    norm_scale = 1.0 / math.sqrt(vol_count * nar_count * slot_total)
    facing = directions(observer_cells)
    share_rows = bin_cap // vol_count
    regrouped = lax.all_to_all(spectra, "vol", split_axis=0, concat_axis=2, tiled=True)
    bin_ids = own_start + vol_index * share_rows + jnp.arange(share_rows, dtype=jnp.int32)
    span_points = local_points * max(1, vol_count // 8)
    turn_count = vol_count * local_points // span_points

    def add_block(turn_index, running):
        first_point = turn_index * span_points
        spec_block = lax.dynamic_slice_in_dim(regrouped, first_point, span_points, 2)
        flat_index = first_point + jnp.arange(span_points, dtype=jnp.int32)
        point_list = point_ids(flat_index // local_points, flat_index % local_points)
        dotted = project(facing, positions(point_list))
        return running + apply_green(bin_ids, spec_block, dotted, facing, norm_scale)

    result = lax.fori_loop(
        0, turn_count, add_block, jnp.zeros((share_rows, 2, observer_cells.shape[1]), jnp.float32)
    )
    return result.reshape(1, share_rows, 2, result.shape[-1])


def solution(mesh):
    placed = (P(("vol", "nar"), None), P("vol", "nar", None), P(), P())
    return jax.shard_map(
        per_device,
        mesh=mesh,
        in_specs=placed,
        out_specs=P("nar", "vol", None, None),
        check_vma=False,
    )
```

profile of v0, /device:TPU:0, one launch (start us, length us, event | category | flops | bytes accessed | tf_op | source)
XLA Modules:
  0.0 133.8 jit_solution(10418153351370994909)
XLA Ops:
  0.0 0.7 compare_reduce_fusion
  0.7 0.7 maximum_bitcast_fusion
  1.6 0.6 gather_fusion
  2.2 0.8 broadcast_select_fusion.1
  3.0 7.3 %all-to-all-start = ((bf16[8,2,2048]{2,1,0:T(2,128)(2,1)}), bf16[8,2,2048]{2,1,0:T(2,128)(2,1)S(1)}, u32[]{:S(2)}, u32[]{:S(2)}) async-start(bf16[8,2,2048]{2,1,0:T(2,128)(2,1)} %broadcast_select_fusion.1), calls=%async_computation | async-start | bytes 131072 | tf_op jit(solution)/shard_map/all_to_all | solution.py:84
  10.3 0.8 reduce-window.9
  11.1 0.7 bitcast_subtract_fusion
  11.8 1.3 dynamic_slice.18
  13.0 0.7 dynamic_slice.17
  13.7 0.7 add_add_fusion
  14.4 1.1 fusion.36
  15.5 0.6 iota_compare_fusion
  16.2 0.2 copy.26
  16.5 0.7 all-to-all-done
  17.2 5.8 %all_gather.3 = bf16[64,2048]{1,0:T(8,128)(2,1)S(1)} all-gather(bf16[16,2048]{1,0:T(8,128)(2,1)S(1)} %all_to_all.20), channel_id=1, replica_groups=mesh['vol'=8,'nar'=4] {'nar'}, dimensions={0}, use_global_device_ids=true | all-gather | bytes 327680 | tf_op jit(solution)/shard_map/all_gather | solution.py:91
  23.0 0.2 reshape.597
  23.2 0.3 fusion.28
  23.5 10.0 %reshape.598 = bf16[64,4,128,2]{1,0,3,2:T(8,128)(2,1)} reshape(bf16[256,256]{0,1:T(8,128)(2,1)S(1)} %copy.27) | data formatting | bytes 262144 | tf_op jit(solution)/shard_map/reshape | solution.py:96
  33.5 6.2 %copy.28 = bf16[128,4,2,64]{0,3,2,1:T(8,128)(2,1)S(1)} copy(bf16[128,4,2,64]{1,3,2,0:T(8,128)(2,1)} %bitcast.64) | data formatting | bytes 262144 | tf_op jit(solution)/shard_map/transpose | solution.py:97
  39.7 0.2 copy.29
  39.9 0.9 reshape.631
  40.8 5.4 %all-to-all-start.1 = ((bf16[8,2,4096]{2,1,0:T(2,128)(2,1)}), bf16[8,2,4096]{2,1,0:T(2,128)(2,1)S(1)}, u32[]{:S(2)}, u32[]{:S(2)}) async-start(bf16[8,2,4096]{2,1,0:T(2,128)(2,1)} %reshape.631), calls=%async_computation.1 | async-start | bytes 262144 | tf_op jit(solution)/shard_map/all_to_all | solution.py:112
  47.0 6.6 %all-to-all-done.1 = bf16[8,2,4096]{2,1,0:T(2,128)(2,1)S(1)} async-done(((bf16[8,2,4096]{2,1,0:T(2,128)(2,1)}), bf16[8,2,4096]{2,1,0:T(2,128)(2,1)S(1)}, u32[]{:S(2)}, u32[]{:S(2)}) %all-to-all-start.1) | async-done | bytes 131104 | tf_op jit(solution)/shard_map/all_to_all | solution.py:112
  53.7 0.2 reshape.632
  53.9 0.2 copy.30
  54.1 0.2 all_to_all.24
  54.3 78.9 %while.19 = (s32[]{:T(128)}, f32[16,2,512]{2,1,0:T(2,128)S(1)}, f32[512]{0:T(512)S(1)}, f32[512]{0:T(512)S(1)}, f32[512]{0:T(512)S(1)}, /*index=5*/bf16[16,8,512...) while((s32[]{:T(128)}, f32[16,2,512]{2,1,0:T(2,128)S(1)}, ...), condition=%wide.region_4.5_spmd.clone.clone.clone, body=%wide.region_1.4_spmd.clone.clone.clone.sunk | while | flops 22971540 | bytes 8845429 | solution.py:125
  54.6 7.8 %fusion.56 = (bf16[16,512,64]{1,2,0:T(8,128)(2,1)S(1)}, bf16[16,512,64]{1,2,0:T(8,128)(2,1)S(1)}) fusion(f32[512,64]{0,1:T(8,128)S(1)} %multiply_add_fusion.2, f32[16]{0:T(128)S(1)} %fusion.55), kind=kLoop, calls=%fused_computation.5.clone.1 | loop fusion | flops 1572864 | bytes 2228288 | tf_op jit(solution)/shard_map/convert
  62.4 0.4 fusion.57
  62.9 0.1 reshape.635
  63.0 0.1 reshape.636
  63.2 0.3 slice_add_fusion.2
  63.6 0.2 fusion.59
  64.5 7.8 %fusion.56 = (bf16[16,512,64]{1,2,0:T(8,128)(2,1)S(1)}, bf16[16,512,64]{1,2,0:T(8,128)(2,1)S(1)}) fusion(f32[512,64]{0,1:T(8,128)S(1)} %multiply_add_fusion.2, f32[16]{0:T(128)S(1)} %fusion.55), kind=kLoop, calls=%fused_computation.5.clone.1 | loop fusion | flops 1572864 | bytes 2228288 | tf_op jit(solution)/shard_map/convert
  72.2 0.4 fusion.57
  73.0 0.3 slice_add_fusion.2
  73.5 0.2 fusion.59
  74.3 7.8 %fusion.56 = (bf16[16,512,64]{1,2,0:T(8,128)(2,1)S(1)}, bf16[16,512,64]{1,2,0:T(8,128)(2,1)S(1)}) fusion(f32[512,64]{0,1:T(8,128)S(1)} %multiply_add_fusion.2, f32[16]{0:T(128)S(1)} %fusion.55), kind=kLoop, calls=%fused_computation.5.clone.1 | loop fusion | flops 1572864 | bytes 2228288 | tf_op jit(solution)/shard_map/convert
  82.1 0.4 fusion.57
  82.9 0.3 slice_add_fusion.2
  83.3 0.2 fusion.59
  84.2 7.8 %fusion.56 = (bf16[16,512,64]{1,2,0:T(8,128)(2,1)S(1)}, bf16[16,512,64]{1,2,0:T(8,128)(2,1)S(1)}) fusion(f32[512,64]{0,1:T(8,128)S(1)} %multiply_add_fusion.2, f32[16]{0:T(128)S(1)} %fusion.55), kind=kLoop, calls=%fused_computation.5.clone.1 | loop fusion | flops 1572864 | bytes 2228288 | tf_op jit(solution)/shard_map/convert
  92.0 0.4 fusion.57
  92.8 0.3 slice_add_fusion.2
  93.2 0.2 fusion.59
  94.1 7.8 %fusion.56 = (bf16[16,512,64]{1,2,0:T(8,128)(2,1)S(1)}, bf16[16,512,64]{1,2,0:T(8,128)(2,1)S(1)}) fusion(f32[512,64]{0,1:T(8,128)S(1)} %multiply_add_fusion.2, f32[16]{0:T(128)S(1)} %fusion.55), kind=kLoop, calls=%fused_computation.5.clone.1 | loop fusion | flops 1572864 | bytes 2228288 | tf_op jit(solution)/shard_map/convert
  101.8 0.4 fusion.57
  102.6 0.3 slice_add_fusion.2
  103.1 0.2 fusion.59
  103.9 7.8 %fusion.56 = (bf16[16,512,64]{1,2,0:T(8,128)(2,1)S(1)}, bf16[16,512,64]{1,2,0:T(8,128)(2,1)S(1)}) fusion(f32[512,64]{0,1:T(8,128)S(1)} %multiply_add_fusion.2, f32[16]{0:T(128)S(1)} %fusion.55), kind=kLoop, calls=%fused_computation.5.clone.1 | loop fusion | flops 1572864 | bytes 2228288 | tf_op jit(solution)/shard_map/convert
  111.7 0.4 fusion.57
  112.4 0.1 reshape.636
  112.5 0.3 slice_add_fusion.2
  112.9 0.2 fusion.59
  113.8 7.8 %fusion.56 = (bf16[16,512,64]{1,2,0:T(8,128)(2,1)S(1)}, bf16[16,512,64]{1,2,0:T(8,128)(2,1)S(1)}) fusion(f32[512,64]{0,1:T(8,128)S(1)} %multiply_add_fusion.2, f32[16]{0:T(128)S(1)} %fusion.55), kind=kLoop, calls=%fused_computation.5.clone.1 | loop fusion | flops 1572864 | bytes 2228288 | tf_op jit(solution)/shard_map/convert
  121.6 0.4 fusion.57
  122.1 0.1 reshape.635
  122.4 0.3 slice_add_fusion.2
  122.8 0.2 fusion.59
  123.6 7.8 %fusion.56 = (bf16[16,512,64]{1,2,0:T(8,128)(2,1)S(1)}, bf16[16,512,64]{1,2,0:T(8,128)(2,1)S(1)}) fusion(f32[512,64]{0,1:T(8,128)S(1)} %multiply_add_fusion.2, f32[16]{0:T(128)S(1)} %fusion.55), kind=kLoop, calls=%fused_computation.5.clone.1 | loop fusion | flops 1572864 | bytes 2228288 | tf_op jit(solution)/shard_map/convert
  131.4 0.4 fusion.57
  132.2 0.3 slice_add_fusion.2
  132.7 0.2 fusion.59
  133.2 0.6 copy-done.1
  (123 shorter events, 8.1 us)
Async XLA Ops:
  0.0 1.6 %copy-start = (bf16[64,2048]{1,0:T(8,128)(2,1)S(1)}, bf16[64,2048]{1,0:T(8,128)(2,1)}, u32[]{:S(2)}) copy-start(bf16[64,2048]{1,0:T(8,128)(2,1)} %param.6) | copy-start | bytes 786436
  3.0 14.2 %all-to-all-start = ((bf16[8,2,2048]{2,1,0:T(2,128)(2,1)}), bf16[8,2,2048]{2,1,0:T(2,128)(2,1)S(1)}, u32[]{:S(2)}, u32[]{:S(2)}) async-start(bf16[8,2,2048]{2,1,0:T(2,128)(2,1)} %broadcast_select_fusion.1), calls=%async_computation | async-start | bytes 131072 | tf_op jit(solution)/shard_map/all_to_all | solution.py:84
  33.5 13.4 %copy-start.2 = (s32[2,512]{1,0:T(2,128)S(1)}, s32[2,512]{1,0:T(2,128)}, u32[]{:S(2)}) copy-start(s32[2,512]{1,0:T(2,128)} %param.9) | copy-start | bytes 12292
  40.8 12.9 %all-to-all-start.1 = ((bf16[8,2,4096]{2,1,0:T(2,128)(2,1)}), bf16[8,2,4096]{2,1,0:T(2,128)(2,1)S(1)}, u32[]{:S(2)}, u32[]{:S(2)}) async-start(bf16[8,2,4096]{2,1,0:T(2,128)(2,1)} %reshape.631), calls=%async_computation.1 | async-start | bytes 262144 | tf_op jit(solution)/shard_map/all_to_all | solution.py:112
  133.2 0.6 copy-start.1
where the time goes:
time: 134 us
  other arithmetic  78 us (58%)
  local copies, waits for them, and re-layouts  24.5 us (18%)
  starting transfers between devices  12.6 us (9%)
  waiting for transfers between devices  7.29 us (5%)
  blocking collectives  5.78 us (4%)
  matrix products  3.81 us (3%)
    another operation x9, other arithmetic  63 us
    reshape x1, local copies, waits for them, and re-layouts, per_device(): (spectral * dft_scale).astype(jnp.bfloat16)  9.98 us
    all_to_all x1, starting transfers between devices, per_device(): lax.all_to_all(packed, 'vol', split_axis=0, concat_axis=0, tiled=True)  7.28 us
    all_to_all x1, waiting for transfers between devices, per_device(): lax.all_to_all(spectra, 'vol', split_axis=0, concat_axis=2, tiled=True)  6.64 us
    transpose x1, local copies, waits for them, and re-layouts, per_device(): spectra = spectral.transpose(2, 1, 3, 0).reshape(bin_cap, 2 * NQ, rows_here)  6.2 us
    all_gather x1, blocking collectives, per_device(): row_piece = lax.all_gather(arrived, 'nar', axis=0, tiled=True)  5.78 us
    all_to_all x1, starting transfers between devices, per_device(): lax.all_to_all(spectra, 'vol', split_axis=0, concat_axis=2, tiled=True)  5.37 us
    dot_general x8, matrix products, apply_green(): jnp.einsum('bxp,bcp->bxc', green_grid, spec_block, preferred_element_type...  3.55 us
  transfers between devices with their start and end apart: 2, of which 2 were waited for; matrix products, arithmetic and copies ran while one was open for 5% of the time, Pallas kernels for 0%

commit v1 on v0

--- a/solution.py
+++ b/solution.py
@@ -109,7 +109,18 @@
     norm_scale = 1.0 / math.sqrt(vol_count * nar_count * slot_total)
     facing = directions(observer_cells)
     share_rows = bin_cap // vol_count
-    regrouped = lax.all_to_all(spectra, "vol", split_axis=0, concat_axis=2, tiled=True)
+    ways, here = (lax.axis_size("vol"), lax.axis_index("vol"))
+    width = spectra.shape[0] // ways
+    shape = list(spectra.shape)
+    shape[0] = width
+    height = shape[2]
+    shape[2] = height * ways
+    regrouped = jnp.zeros(shape, spectra.dtype)
+    for mask in range(ways):
+        part = lax.dynamic_slice_in_dim(spectra, (here ^ mask) * width, width, axis=0)
+        if mask:
+            part = lax.ppermute(part, "vol", [(d, d ^ mask) for d in range(ways)])
+        regrouped = lax.dynamic_update_slice_in_dim(regrouped, part, (here ^ mask) * height, axis=2)
     bin_ids = own_start + vol_index * share_rows + jnp.arange(share_rows, dtype=jnp.int32)
     span_points = local_points * max(1, vol_count // 8)
     turn_count = vol_count * local_points // span_points

time: 134 us -> 151 us (1.13)
  local copies, waits for them, and re-layouts: 24.5 us -> 35.4 us
  starting transfers between devices: 12.6 us -> 18.2 us
    dynamic_update_slice x0 -> x8, local copies, waits for them, and re-layouts: none -> 11.3 us  [per_device(): lax.dynamic_update_slice_in_dim(regrouped, part, (here ^ mask) * height,...]
    ppermute x0 -> x7, starting transfers between devices: none -> 11 us  [per_device(): part = lax.ppermute(part, 'vol', [(d, d ^ mask) for d in range(ways)])]
    all_to_all x1 -> x0, waiting for transfers between devices: 6.64 us -> none  [per_device(): lax.all_to_all(spectra, 'vol', split_axis=0, concat_axis=2, tiled=True)]
    ppermute x0 -> x7, waiting for transfers between devices: none -> 6.45 us  [per_device(): part = lax.ppermute(part, 'vol', [(d, d ^ mask) for d in range(ways)])]
    all_to_all x1 -> x0, starting transfers between devices: 5.37 us -> none  [per_device(): lax.all_to_all(spectra, 'vol', split_axis=0, concat_axis=2, tiled=True)]
  transfers between devices with their start and end apart: 2 -> 8, of which waited for: 2 -> 3; matrix products, arithmetic and copies ran while one was open for 5% -> 10% of each run, Pallas kernels for 0% -> 0%
where the time goes in v1:
time: 151 us; the launch traced here: 150 us
  other arithmetic  77.9 us (52%)
  local copies, waits for them, and re-layouts  35.4 us (23%)
  starting transfers between devices  18.2 us (12%)
  waiting for transfers between devices  7.26 us (5%)
  blocking collectives  5.78 us (4%)
  matrix products  3.81 us (3%)
    another operation x9, other arithmetic  63 us
    dynamic_update_slice x8, local copies, waits for them, and re-layouts, per_device(): lax.dynamic_update_slice_in_dim(regrouped, part, (here ^ mask) * height,...  11.3 us
    ppermute x7, starting transfers between devices, per_device(): part = lax.ppermute(part, 'vol', [(d, d ^ mask) for d in range(ways)])  11 us
    reshape x1, local copies, waits for them, and re-layouts, per_device(): (spectral * dft_scale).astype(jnp.bfloat16)  9.98 us
    all_to_all x1, starting transfers between devices, per_device(): lax.all_to_all(packed, 'vol', split_axis=0, concat_axis=0, tiled=True)  7.28 us
    ppermute x7, waiting for transfers between devices, per_device(): part = lax.ppermute(part, 'vol', [(d, d ^ mask) for d in range(ways)])  6.45 us
    transpose x1, local copies, waits for them, and re-layouts, per_device(): spectra = spectral.transpose(2, 1, 3, 0).reshape(bin_cap, 2 * NQ, rows_here)  6.19 us
    all_gather x1, blocking collectives, per_device(): row_piece = lax.all_gather(arrived, 'nar', axis=0, tiled=True)  5.78 us
  transfers between devices with their start and end apart: 8, of which 3 were waited for; matrix products, arithmetic and copies ran while one was open for 10% of the time, Pallas kernels for 0%

profile of v1, /device:TPU:0, one launch (start us, length us, event | category | flops | bytes accessed | tf_op | source)
XLA Modules:
  0.0 150.3 jit_solution(2405852489423786159)
XLA Ops:
  0.0 0.7 compare_reduce_fusion
  0.7 0.7 maximum_bitcast_fusion
  1.6 0.6 gather_fusion
  2.2 0.8 broadcast_select_fusion.1
  3.0 7.3 %all-to-all-start = ((bf16[8,2,2048]{2,1,0:T(2,128)(2,1)}), bf16[8,2,2048]{2,1,0:T(2,128)(2,1)S(1)}, u32[]{:S(2)}, u32[]{:S(2)}) async-start(bf16[8,2,2048]{2,1,0:T(2,128)(2,1)} %broadcast_select_fusion.1), calls=%async_computation | async-start | bytes 131072 | tf_op jit(solution)/shard_map/all_to_all | solution.py:84
  10.3 0.8 reduce-window.9
  11.1 0.7 bitcast_subtract_fusion
  11.8 1.2 dynamic_slice.42
  13.0 0.6 dynamic_slice.41
  13.6 0.6 add_add_fusion
  14.2 1.1 fusion.36
  15.4 0.6 iota_compare_fusion
  16.4 0.8 all-to-all-done
  17.2 5.8 %all_gather.3 = bf16[64,2048]{1,0:T(8,128)(2,1)S(1)} all-gather(bf16[16,2048]{1,0:T(8,128)(2,1)S(1)} %all_to_all.7), channel_id=1, replica_groups=mesh['vol'=8,'nar'=4] {'nar'}, dimensions={0}, use_global_device_ids=true | all-gather | bytes 327680 | tf_op jit(solution)/shard_map/all_gather | solution.py:91
  23.2 0.3 fusion.28
  23.5 10.0 %reshape.598 = bf16[64,4,128,2]{1,0,3,2:T(8,128)(2,1)} reshape(bf16[256,256]{0,1:T(8,128)(2,1)S(1)} %copy.26) | data formatting | bytes 262144 | tf_op jit(solution)/shard_map/reshape | solution.py:96
  33.5 6.2 %copy.27 = bf16[128,4,2,64]{0,3,2,1:T(8,128)(2,1)S(1)} copy(bf16[128,4,2,64]{1,3,2,0:T(8,128)(2,1)} %bitcast.59) | data formatting | bytes 262144 | tf_op jit(solution)/shard_map/transpose | solution.py:97
  39.7 0.4 constant_dynamic-slice_fusion
  40.2 1.3 collective-permute-start
  41.5 1.5 collective-permute-start.1
  42.9 0.8 collective-permute-start.2
  43.7 2.1 %collective-permute-start.3 = (bf16[16,8,64]{0,2,1:T(8,128)(2,1)S(1)}, bf16[16,8,64]{0,2,1:T(8,128)(2,1)S(1)}, u32[]{:S(2)}, u32[]{:S(2)}) collective-permute-start(bf16[16,8,64]{0,2,1:T(8,128)(2,1)S(1)} %get-tuple-element.352), channel_id=1, source_target_pairs={{0,16},{4,20},{8,24},{12,28},{16,0},{20,4},{24,8},{28,12},{1,17},{... | collective-permute-start | bytes 49160 | tf_op jit(solution)/shard_map/ppermute | solution.py:122
  45.8 1.5 collective-permute-start.4
  47.3 3.3 %collective-permute-start.5 = (bf16[16,8,64]{0,2,1:T(8,128)(2,1)S(1)}, bf16[16,8,64]{0,2,1:T(8,128)(2,1)S(1)}, u32[]{:S(2)}, u32[]{:S(2)}) collective-permute-start(bf16[16,8,64]{0,2,1:T(8,128)(2,1)S(1)} %get-tuple-element.350), channel_id=1, source_target_pairs={{0,24},{4,28},{8,16},{12,20},{16,8},{20,12},{24,0},{28,4},{1,25},{... | collective-permute-start | bytes 49160 | tf_op jit(solution)/shard_map/ppermute | solution.py:122
  50.6 1.7 %collective-permute-done.1 = bf16[16,8,64]{0,2,1:T(8,128)(2,1)S(1)} collective-permute-done((bf16[16,8,64]{0,2,1:T(8,128)(2,1)S(1)}, bf16[16,8,64]{0,2,1:T(8,128)(2,1)S(1)}, u32[]{:S(2)}, u32[]{:S(2)}) %collective-permute-start.1) | collective-permute-done | bytes 16416 | tf_op jit(solution)/shard_map/ppermute | solution.py:122
  52.3 0.6 collective-permute-start.6
  53.8 0.3 dynamic_update_slice.24
  54.3 2.5 %dynamic_update_slice.25 = bf16[16,8,512]{2,1,0:T(8,128)(2,1)S(1)} dynamic-update-slice(bf16[16,8,512]{2,1,0:T(8,128)(2,1)S(1)} %dynamic_update_slice.24, bf16[16,8,64]{2,1,0:T(8,128)(2,1)S(1)} %copy.29, s32[]{:T(128)} %constant.416.clone.1, s32[]{:T(128)} %constant.416.clone.1, s32[]{:T(128)S(6)} %select_n.392) | dynamic-update-slice | bytes 32772 | tf_op jit(solution)/shard_map/dynamic_update_slice | solution.py:123
  56.9 0.3 dynamic_update_slice.26
  57.4 2.5 %dynamic_update_slice.27 = bf16[16,8,512]{2,1,0:T(8,128)(2,1)S(1)} dynamic-update-slice(bf16[16,8,512]{2,1,0:T(8,128)(2,1)S(1)} %dynamic_update_slice.26, bf16[16,8,64]{2,1,0:T(8,128)(2,1)S(1)} %copy.31, s32[]{:T(128)} %constant.416.clone.1, s32[]{:T(128)} %constant.416.clone.1, s32[]{:T(128)S(6)} %select_n.396) | dynamic-update-slice | bytes 32772 | tf_op jit(solution)/shard_map/dynamic_update_slice | solution.py:123
  60.0 0.3 dynamic_update_slice.28
  60.4 4.7 %collective-permute-done.4 = bf16[16,8,64]{0,2,1:T(8,128)(2,1)S(1)} collective-permute-done((bf16[16,8,64]{0,2,1:T(8,128)(2,1)S(1)}, bf16[16,8,64]{0,2,1:T(8,128)(2,1)S(1)}, u32[]{:S(2)}, u32[]{:S(2)}) %collective-permute-start.4) | collective-permute-done | bytes 16416 | tf_op jit(solution)/shard_map/ppermute | solution.py:122
  65.2 2.5 %dynamic_update_slice.29 = bf16[16,8,512]{2,1,0:T(8,128)(2,1)S(1)} dynamic-update-slice(bf16[16,8,512]{2,1,0:T(8,128)(2,1)S(1)} %dynamic_update_slice.28, bf16[16,8,64]{2,1,0:T(8,128)(2,1)S(1)} %copy.33, s32[]{:T(128)} %constant.416.clone.1, s32[]{:T(128)} %constant.416.clone.1, s32[]{:T(128)S(6)} %select_n.400) | dynamic-update-slice | bytes 32772 | tf_op jit(solution)/shard_map/dynamic_update_slice | solution.py:123
  67.8 0.3 dynamic_update_slice.30
  68.3 2.5 %dynamic_update_slice.31 = bf16[16,8,512]{2,1,0:T(8,128)(2,1)S(1)} dynamic-update-slice(bf16[16,8,512]{2,1,0:T(8,128)(2,1)S(1)} %dynamic_update_slice.30, bf16[16,8,64]{2,1,0:T(8,128)(2,1)S(1)} %copy.35, s32[]{:T(128)} %constant.416.clone.1, s32[]{:T(128)} %constant.416.clone.1, s32[]{:T(128)S(6)} %select_n.404) | dynamic-update-slice | bytes 32772 | tf_op jit(solution)/shard_map/dynamic_update_slice | solution.py:123
  70.8 78.9 %while.19 = (s32[]{:T(128)}, f32[16,2,512]{2,1,0:T(2,128)S(1)}, f32[512]{0:T(512)S(1)}, f32[512]{0:T(512)S(1)}, f32[512]{0:T(512)S(1)}, /*index=5*/bf16[16,8,512...) while((s32[]{:T(128)}, f32[16,2,512]{2,1,0:T(2,128)S(1)}, ...), condition=%wide.region_4.5_spmd.clone.clone.clone, body=%wide.region_1.4_spmd.clone.clone.clone.sunk | while | flops 22971540 | bytes 8845429 | solution.py:136
  71.1 7.8 %fusion.56 = (bf16[16,512,64]{1,2,0:T(8,128)(2,1)S(1)}, bf16[16,512,64]{1,2,0:T(8,128)(2,1)S(1)}) fusion(f32[512,64]{0,1:T(8,128)S(1)} %multiply_add_fusion.2, f32[16]{0:T(128)S(1)} %fusion.55), kind=kLoop, calls=%fused_computation.5.clone.1 | loop fusion | flops 1572864 | bytes 2228288 | tf_op jit(solution)/shard_map/convert
  78.9 0.4 fusion.57
  79.7 0.3 slice_add_fusion.2
  80.1 0.2 fusion.59
  80.9 7.8 %fusion.56 = (bf16[16,512,64]{1,2,0:T(8,128)(2,1)S(1)}, bf16[16,512,64]{1,2,0:T(8,128)(2,1)S(1)}) fusion(f32[512,64]{0,1:T(8,128)S(1)} %multiply_add_fusion.2, f32[16]{0:T(128)S(1)} %fusion.55), kind=kLoop, calls=%fused_computation.5.clone.1 | loop fusion | flops 1572864 | bytes 2228288 | tf_op jit(solution)/shard_map/convert
  88.7 0.4 fusion.57
  89.5 0.3 slice_add_fusion.2
  90.8 7.8 %fusion.56 = (bf16[16,512,64]{1,2,0:T(8,128)(2,1)S(1)}, bf16[16,512,64]{1,2,0:T(8,128)(2,1)S(1)}) fusion(f32[512,64]{0,1:T(8,128)S(1)} %multiply_add_fusion.2, f32[16]{0:T(128)S(1)} %fusion.55), kind=kLoop, calls=%fused_computation.5.clone.1 | loop fusion | flops 1572864 | bytes 2228288 | tf_op jit(solution)/shard_map/convert
  98.6 0.4 fusion.57
  99.4 0.3 slice_add_fusion.2
  99.8 0.2 fusion.59
  100.7 7.8 %fusion.56 = (bf16[16,512,64]{1,2,0:T(8,128)(2,1)S(1)}, bf16[16,512,64]{1,2,0:T(8,128)(2,1)S(1)}) fusion(f32[512,64]{0,1:T(8,128)S(1)} %multiply_add_fusion.2, f32[16]{0:T(128)S(1)} %fusion.55), kind=kLoop, calls=%fused_computation.5.clone.1 | loop fusion | flops 1572864 | bytes 2228288 | tf_op jit(solution)/shard_map/convert
  108.5 0.4 fusion.57
  109.3 0.3 slice_add_fusion.2
  109.7 0.2 fusion.59
  110.5 7.8 %fusion.56 = (bf16[16,512,64]{1,2,0:T(8,128)(2,1)S(1)}, bf16[16,512,64]{1,2,0:T(8,128)(2,1)S(1)}) fusion(f32[512,64]{0,1:T(8,128)S(1)} %multiply_add_fusion.2, f32[16]{0:T(128)S(1)} %fusion.55), kind=kLoop, calls=%fused_computation.5.clone.1 | loop fusion | flops 1572864 | bytes 2228288 | tf_op jit(solution)/shard_map/convert
  118.3 0.4 fusion.57
  119.1 0.3 slice_add_fusion.2
  120.4 7.8 %fusion.56 = (bf16[16,512,64]{1,2,0:T(8,128)(2,1)S(1)}, bf16[16,512,64]{1,2,0:T(8,128)(2,1)S(1)}) fusion(f32[512,64]{0,1:T(8,128)S(1)} %multiply_add_fusion.2, f32[16]{0:T(128)S(1)} %fusion.55), kind=kLoop, calls=%fused_computation.5.clone.1 | loop fusion | flops 1572864 | bytes 2228288 | tf_op jit(solution)/shard_map/convert
  128.2 0.4 fusion.57
  129.0 0.3 slice_add_fusion.2
  130.3 7.8 %fusion.56 = (bf16[16,512,64]{1,2,0:T(8,128)(2,1)S(1)}, bf16[16,512,64]{1,2,0:T(8,128)(2,1)S(1)}) fusion(f32[512,64]{0,1:T(8,128)S(1)} %multiply_add_fusion.2, f32[16]{0:T(128)S(1)} %fusion.55), kind=kLoop, calls=%fused_computation.5.clone.1 | loop fusion | flops 1572864 | bytes 2228288 | tf_op jit(solution)/shard_map/convert
  138.1 0.4 fusion.57
  138.9 0.3 slice_add_fusion.2
  140.1 7.8 %fusion.56 = (bf16[16,512,64]{1,2,0:T(8,128)(2,1)S(1)}, bf16[16,512,64]{1,2,0:T(8,128)(2,1)S(1)}) fusion(f32[512,64]{0,1:T(8,128)S(1)} %multiply_add_fusion.2, f32[16]{0:T(128)S(1)} %fusion.55), kind=kLoop, calls=%fused_computation.5.clone.1 | loop fusion | flops 1572864 | bytes 2228288 | tf_op jit(solution)/shard_map/convert
  147.9 0.4 fusion.57
  148.7 0.3 slice_add_fusion.2
  149.7 0.6 copy-done.1
  (148 shorter events, 10.9 us)
Async XLA Ops:
  0.0 1.6 %copy-start = (bf16[64,2048]{1,0:T(8,128)(2,1)S(1)}, bf16[64,2048]{1,0:T(8,128)(2,1)}, u32[]{:S(2)}) copy-start(bf16[64,2048]{1,0:T(8,128)(2,1)} %param.6) | copy-start | bytes 786436
  3.0 14.2 %all-to-all-start = ((bf16[8,2,2048]{2,1,0:T(2,128)(2,1)}), bf16[8,2,2048]{2,1,0:T(2,128)(2,1)S(1)}, u32[]{:S(2)}, u32[]{:S(2)}) async-start(bf16[8,2,2048]{2,1,0:T(2,128)(2,1)} %broadcast_select_fusion.1), calls=%async_computation | async-start | bytes 131072 | tf_op jit(solution)/shard_map/all_to_all | solution.py:84
  39.7 13.2 %copy-start.2 = (s32[2,512]{1,0:T(2,128)S(1)}, s32[2,512]{1,0:T(2,128)}, u32[]{:S(2)}) copy-start(s32[2,512]{1,0:T(2,128)} %param.9) | copy-start | bytes 12292
  40.2 7.1 %collective-permute-start = (bf16[16,8,64]{0,2,1:T(8,128)(2,1)S(1)}, bf16[16,8,64]{0,2,1:T(8,128)(2,1)S(1)}, u32[]{:S(2)}, u32[]{:S(2)}) collective-permute-start(bf16[16,8,64]{0,2,1:T(8,128)(2,1)S(1)} %get-tuple-element.355), channel_id=1, source_target_pairs={{0,4},{4,0},{8,12},{12,8},{16,20},{20,16},{24,28},{28,24},{1,5},{5... | collective-permute-start | bytes 49160 | tf_op jit(solution)/shard_map/ppermute | solution.py:122
  41.5 10.9 %collective-permute-start.1 = (bf16[16,8,64]{0,2,1:T(8,128)(2,1)S(1)}, bf16[16,8,64]{0,2,1:T(8,128)(2,1)S(1)}, u32[]{:S(2)}, u32[]{:S(2)}) collective-permute-start(bf16[16,8,64]{0,2,1:T(8,128)(2,1)S(1)} %get-tuple-element.354), channel_id=1, source_target_pairs={{0,8},{4,12},{8,0},{12,4},{16,24},{20,28},{24,16},{28,20},{1,9},{5... | collective-permute-start | bytes 49160 | tf_op jit(solution)/shard_map/ppermute | solution.py:122
  42.9 14.4 %collective-permute-start.2 = (bf16[16,8,64]{0,2,1:T(8,128)(2,1)S(1)}, bf16[16,8,64]{0,2,1:T(8,128)(2,1)S(1)}, u32[]{:S(2)}, u32[]{:S(2)}) collective-permute-start(bf16[16,8,64]{0,2,1:T(8,128)(2,1)S(1)} %get-tuple-element.353), channel_id=1, source_target_pairs={{0,12},{4,8},{8,4},{12,0},{16,28},{20,24},{24,20},{28,16},{1,13},{... | collective-permute-start | bytes 49160 | tf_op jit(solution)/shard_map/ppermute | solution.py:122
  43.7 16.2 %collective-permute-start.3 = (bf16[16,8,64]{0,2,1:T(8,128)(2,1)S(1)}, bf16[16,8,64]{0,2,1:T(8,128)(2,1)S(1)}, u32[]{:S(2)}, u32[]{:S(2)}) collective-permute-start(bf16[16,8,64]{0,2,1:T(8,128)(2,1)S(1)} %get-tuple-element.352), channel_id=1, source_target_pairs={{0,16},{4,20},{8,24},{12,28},{16,0},{20,4},{24,8},{28,12},{1,17},{... | collective-permute-start | bytes 49160 | tf_op jit(solution)/shard_map/ppermute | solution.py:122
  45.8 19.2 %collective-permute-start.4 = (bf16[16,8,64]{0,2,1:T(8,128)(2,1)S(1)}, bf16[16,8,64]{0,2,1:T(8,128)(2,1)S(1)}, u32[]{:S(2)}, u32[]{:S(2)}) collective-permute-start(bf16[16,8,64]{0,2,1:T(8,128)(2,1)S(1)} %get-tuple-element.351), channel_id=1, source_target_pairs={{0,20},{4,16},{8,28},{12,24},{16,4},{20,0},{24,12},{28,8},{1,21},{... | collective-permute-start | bytes 49160 | tf_op jit(solution)/shard_map/ppermute | solution.py:122
  47.3 20.4 %collective-permute-start.5 = (bf16[16,8,64]{0,2,1:T(8,128)(2,1)S(1)}, bf16[16,8,64]{0,2,1:T(8,128)(2,1)S(1)}, u32[]{:S(2)}, u32[]{:S(2)}) collective-permute-start(bf16[16,8,64]{0,2,1:T(8,128)(2,1)S(1)} %get-tuple-element.350), channel_id=1, source_target_pairs={{0,24},{4,28},{8,16},{12,20},{16,8},{20,12},{24,0},{28,4},{1,25},{... | collective-permute-start | bytes 49160 | tf_op jit(solution)/shard_map/ppermute | solution.py:122
  52.3 15.8 %collective-permute-start.6 = (bf16[16,8,64]{0,2,1:T(8,128)(2,1)S(1)}, bf16[16,8,64]{0,2,1:T(8,128)(2,1)S(1)}, u32[]{:S(2)}, u32[]{:S(2)}) collective-permute-start(bf16[16,8,64]{0,2,1:T(8,128)(2,1)S(1)} %get-tuple-element.349), channel_id=1, source_target_pairs={{0,28},{4,24},{8,20},{12,16},{16,12},{20,8},{24,4},{28,0},{1,29},{... | collective-permute-start | bytes 49160 | tf_op jit(solution)/shard_map/ppermute | solution.py:122
  149.7 0.6 copy-start.1
